TPU v7x, 32 devices: a whole 2x2x4 slice. The times are simulated.
32 devices in a mesh: req: 8 (over y, x, core), cand: 4 (over z).
Axes of the slice: x: 2, y: 2, z: 4, core: 2. Of those that a mesh axis runs over, the one named last changes fastest.
Arguments:
- history: bfloat16 [64, 256, 1024], P('req', 'cand'), may hold values from -6 to 6
- history_length: int32 [64], P('req'), may hold values from 32 to 256
- candidate_count: int32 [64], P('req'), may hold values from 512 to 4096
- block_shard: int32 [64, 32], P('req'), may hold values from 0 to 3, as said below
- block_index: int32 [64, 32], P('req'), may hold values from 0 to 3
- item_table: bfloat16 [16, 128, 1024], P('cand'), may hold values from -6 to 6
- item_ages: int32 [64, 4096], P('req', 'cand'), may hold values from 0 to 336
- history_weight: bfloat16 [1024, 2048], P('req'), may hold values from -0.1875 to 0.1875
- candidate_weight: bfloat16 [1024, 2048], P('req'), may hold values from -0.1875 to 0.1875
- output_weight: bfloat16 [1024, 1024], P('req'), may hold values from -0.1875 to 0.1875
- hidden_weight: bfloat16 [1024, 256], P('req'), may hold values from -0.1875 to 0.1875
- norm_gain: float32 [1024], replicated, may hold values from 0.1 to 1.9
- score_weight: bfloat16 [2, 256], replicated, may hold values from -0.375 to 0.375
Outputs:
- scores: float32 [64, 4096], P('req', 'cand')
Inputs may be any that keep to these rules, and one draw needn't show every extreme that they name: `block_shard`: for each group of 8 consecutive requests (aligned) and each c, the slots j with j // 8 == c of those requests name every shard exactly 16 times.
All inputs are finite; a program needn't handle non-finite values.
Results may differ from a plain program's by a relative error of at most 0.0053.
Values may be sent and summed in bfloat16 or wider, within the bound.
A program may use at most 128 MiB of HBM per device.

v0:
```python
import math

import jax
import jax.numpy as jnp
from jax import lax
from jax.sharding import PartitionSpec as P

HEADS = 8
BLOCK = 128


EPSILON = 1e-05
AGE_SCALE = 48.0


def local(
    history,
    history_length,
    candidate_count,
    block_shard,
    block_index,
    item_table,
    item_ages,
    history_weight,
    candidate_weight,
    output_weight,
    hidden_weight,
    norm_gain,
    score_weight,
):
    proj_history, proj_candidate, proj_output, proj_hidden = (
        lax.all_gather(history_weight, "req", axis=0, tiled=True),
        lax.all_gather(candidate_weight, "req", axis=0, tiled=True),
        lax.all_gather(output_weight, "req", axis=0, tiled=True),
        lax.all_gather(hidden_weight, "req", axis=0, tiled=True),
    )
    shards = lax.axis_size("cand")
    my_shard = lax.axis_index("cand")
    requests, max_blocks = block_shard.shape
    per_scorer = max_blocks // shards
    slot_count = requests * per_scorer
    capacity = slot_count // shards
    model_width = item_table.shape[2]
    head_size = model_width // HEADS
    score_scale = 1.0 / math.sqrt(head_size)
    shard_sets = (
        block_shard.reshape(requests, shards, per_scorer)
        .transpose(1, 0, 2)
        .reshape(shards, slot_count)
    )
    index_sets = (
        block_index.reshape(requests, shards, per_scorer)
        .transpose(1, 0, 2)
        .reshape(shards, slot_count)
    )
    is_mine = (shard_sets == my_shard).astype(jnp.int32)
    before = jnp.cumsum(is_mine, axis=1) - is_mine
    picked = is_mine[:, None, :] * (
        before[:, None, :] == jnp.arange(capacity, dtype=jnp.int32)[None, :, None]
    ).astype(jnp.int32)
    send_ids = jnp.sum(picked * index_sets[:, None, :], axis=2)
    outgoing = item_table[send_ids]
    incoming = lax.all_to_all(outgoing, "cand", split_axis=0, concat_axis=0, tiled=True)
    own_shard = lax.dynamic_index_in_dim(shard_sets, my_shard, 0, keepdims=False)
    matches = (own_shard[:, None] == jnp.arange(shards, dtype=jnp.int32)[None, :]).astype(jnp.int32)
    own_rank = jnp.sum((jnp.cumsum(matches, axis=0) - matches) * matches, axis=1)
    arrived = incoming.reshape(shards * capacity, BLOCK, model_width)[
        own_shard * capacity + own_rank
    ]
    arrived = arrived.reshape(requests, per_scorer, BLOCK, model_width)
    first_block = jnp.zeros((requests,), jnp.int32) + my_shard * per_scorer
    block_number = first_block[:, None] + jnp.arange(per_scorer, dtype=jnp.int32)[None, :]
    live_slots = (block_number * BLOCK < candidate_count[:, None]).reshape(slot_count)
    request_of = jnp.arange(slot_count, dtype=jnp.int32) // per_scorer
    local_pairs = jax.nn.silu(
        jnp.dot(history.reshape(-1, model_width), proj_history, preferred_element_type=jnp.float32)
    ).astype(jnp.bfloat16)
    local_pairs = local_pairs.reshape(requests, -1, 2 * model_width)
    projected = lax.all_gather(local_pairs, "cand", axis=1, tiled=True)
    history_total = projected.shape[1]
    positions = jnp.arange(history_total, dtype=jnp.int32)
    query_weight = proj_candidate[:, :model_width]
    gate_weight = proj_candidate[:, model_width:]

    def score_slot(operands):
        block_rows, request, is_live = operands

        def score_block(block_rows):
            query = jax.nn.silu(
                jnp.dot(block_rows, query_weight, preferred_element_type=jnp.float32)
            ).astype(jnp.bfloat16)
            query = query.reshape(BLOCK, HEADS, head_size)
            pair_rows = lax.dynamic_index_in_dim(projected, request, 0, keepdims=False)
            key_rows = pair_rows[:, :model_width].reshape(history_total, HEADS, head_size)
            value_rows = pair_rows[:, model_width:].reshape(history_total, HEADS, head_size)
            length = lax.dynamic_index_in_dim(history_length, request, 0, keepdims=False)
            scores = (
                jnp.einsum("ihd,phd->hip", query, key_rows, preferred_element_type=jnp.float32)
                * score_scale
            )
            weights = jax.nn.silu(scores) / length.astype(jnp.float32)
            weights = jnp.where(positions[None, None, :] < length, weights, 0.0).astype(
                jnp.bfloat16
            )
            attended = jnp.einsum(
                "hip,phd->ihd", weights, value_rows, preferred_element_type=jnp.float32
            ).reshape(BLOCK, model_width)
            gate = jax.nn.silu(jnp.dot(block_rows, gate_weight, preferred_element_type=jnp.float32))
            center = attended - jnp.mean(attended, axis=-1, keepdims=True)
            spread = jnp.mean(center * center, axis=-1, keepdims=True)
            normed = (center * lax.rsqrt(spread + EPSILON) * norm_gain * gate).astype(jnp.bfloat16)
            merged = (
                jnp.dot(normed, proj_output, preferred_element_type=jnp.float32)
                + block_rows.astype(jnp.float32)
            ).astype(jnp.bfloat16)
            hidden = jax.nn.silu(
                jnp.dot(merged, proj_hidden, preferred_element_type=jnp.float32)
            ).astype(jnp.bfloat16)
            return jnp.einsum("ik,ck->ci", hidden, score_weight, preferred_element_type=jnp.float32)

        def empty_block(block_rows):
            return jnp.zeros((2, BLOCK), jnp.float32)

        return lax.cond(is_live, score_block, empty_block, block_rows)

    logits = lax.map(
        score_slot, (arrived.reshape(slot_count, BLOCK, model_width), request_of, live_slots)
    )
    logits = logits.reshape(requests, per_scorer, 2, BLOCK)
    decays = jnp.exp(
        -item_ages.astype(jnp.float32).reshape(requests, per_scorer, BLOCK) / AGE_SCALE
    )
    blended = decays * logits[:, :, 0] + (1.0 - decays) * logits[:, :, 1]
    row_number = (my_shard * per_scorer + jnp.arange(per_scorer, dtype=jnp.int32))[
        None, :, None
    ] * BLOCK + jnp.arange(BLOCK, dtype=jnp.int32)[None, None, :]
    kept_rows = row_number < candidate_count[:, None, None]
    return jnp.where(kept_rows, blended, 0.0).reshape(requests, per_scorer * BLOCK)


def solution(mesh):
    return jax.shard_map(
        local,
        mesh=mesh,
        in_specs=(
            P("req", "cand", None),
            P("req"),
            P("req"),
            P("req", None),
            P("req", None),
            P("cand", None, None),
            P("req", "cand"),
            P("req", None),
            P("req", None),
            P("req", None),
            P("req", None),
            P(),
            P(),
        ),
        out_specs=P("req", "cand"),
        check_vma=False,
    )
```

profile of v0, /device:TPU:1, one launch (start us, length us, event | category | flops | bytes accessed | tf_op | source)
XLA Modules:
  0.0 1651.8 jit_solution(6157410167003567485)
XLA Ops:
  25.1 23.2 %all-gather.5.cloned.1.call-done = bf16[1024,2048]{1,0:T(8,128)(2,1)} async-done(((bf16[128,2048]{1,0:T(8,128)(2,1)}), bf16[1024,2048]{1,0:T(8,128)(2,1)}) %all-gather.5.cloned.1.call-update) | async-done | bytes 4194320 | tf_op jit(solution)/shard_map/all_gather | solution.py:32
  69.9 19.1 %all-gather.9.cloned.1.call-done = bf16[1024,2048]{1,0:T(8,128)(2,1)} async-done(((bf16[128,2048]{1,0:T(8,128)(2,1)}), bf16[1024,2048]{1,0:T(8,128)(2,1)}) %all-gather.9.cloned.1.call-update) | async-done | bytes 4194320 | tf_op jit(solution)/shard_map/all_gather | solution.py:33
  93.1 277.1 %all-gather.7.cloned.1.call-done = bf16[8,256,2048]{2,0,1:T(8,128)(2,1)} async-done(((bf16[8,64,2048]{2,0,1:T(8,128)(2,1)}), bf16[8,256,2048]{2,0,1:T(8,128)(2,1)}) %all-gather.7.cloned.1.call-update) | async-done | bytes 8388624 | tf_op jit(solution)/shard_map/all_gather | solution.py:79
  382.9 139.5 %all-to-all-done = bf16[4,16,128,1024]{3,2,1,0:T(8,128)(2,1)} async-done(((bf16[4,16,128,1024]{3,2,1,0:T(8,128)(2,1)}), bf16[4,16,128,1024]{3,2,1,0:T(8,128)(2,1)}, u32[]{:S(2)}, u32[]{:S(2)}) %all-to-all-start) | async-done | bytes 16777248 | tf_op jit(solution)/shard_map/all_to_all | solution.py:63
  535.9 1108.1 %while.11 = (s32[]{:T(128)}, f32[64,2,128]{2,1,0:T(2,128)S(1)}, pred[64]{0:T(512)(128)(4,1)S(1)}, bf16[8,256,2048]{1,2,0:T(8,128)(2,1)}, s32[8]{0:T(128)S(1)}, /...) while((s32[]{:T(128)}, f32[64,2,128]{2,1,0:T(2,128)S(1)}, ...), condition=%wide.region_9.10_spmd.clone, body=%wide.region_4.9_spmd.clone.sunk | while | flops 1011778432 | bytes 19286676 | solution.py:126
  537.3 16.0 conditional.3
  554.6 15.9 conditional.3
  571.9 15.9 conditional.3
  589.2 15.9 conditional.3
  606.6 15.9 conditional.3
  623.9 15.9 conditional.3
  641.2 15.9 conditional.3
  658.5 15.9 conditional.3
  675.8 15.9 conditional.3
  693.1 15.9 conditional.3
  710.4 15.9 conditional.3
  727.7 15.9 conditional.3
  745.1 15.9 conditional.3
  762.4 15.9 conditional.3
  779.7 15.9 conditional.3
  797.0 15.9 conditional.3
  814.3 15.9 conditional.3
  1039.4 15.9 conditional.3
  1368.4 15.9 conditional.3
  (1515 shorter events, 1683.8 us)
Async XLA Ops:
  6.5 41.8 %all-gather.5.cloned.1.call-start = ((), (), s32[]{:S(2)}) async-start(), calls=%async_computation.1 | async-start | bytes 4718592 | tf_op jit(solution)/shard_map/all_gather | solution.py:32
  17.0 31.3 %copy-start.7 = (bf16[8,64,1024]{2,1,0:T(8,128)(2,1)S(1)}, bf16[8,64,1024]{2,1,0:T(8,128)(2,1)}, u32[]{:S(2)}) copy-start(bf16[8,64,1024]{2,1,0:T(8,128)(2,1)} %param.17) | copy-start | bytes 3145732
  17.0 505.4 %all-to-all-start = ((bf16[4,16,128,1024]{3,2,1,0:T(8,128)(2,1)}), bf16[4,16,128,1024]{3,2,1,0:T(8,128)(2,1)}, u32[]{:S(2)}, u32[]{:S(2)}) async-start(bf16[4,16,128,1024]{3,2,1,0:T(8,128)(2,1)} %bitcast.105), calls=%async_computation | async-start | bytes 33554432 | tf_op jit(solution)/shard_map/all_to_all | solution.py:63
  24.3 64.7 %all-gather.9.cloned.1.call-start = ((), (), s32[]{:S(2)}) async-start(), calls=%async_computation.3 | async-start | bytes 4718592 | tf_op jit(solution)/shard_map/all_gather | solution.py:33
  25.1 345.1 %all-gather.7.cloned.1.call-start = ((), (), s32[]{:S(2)}) async-start(), calls=%async_computation.2 | async-start | bytes 10485760 | tf_op jit(solution)/shard_map/all_gather | solution.py:79
  55.8 480.1 %all-gather.11.cloned.1.call-start = ((), (), s32[]{:S(2)}) async-start(), calls=%async_computation.4 | async-start | bytes 2359296 | tf_op jit(solution)/shard_map/all_gather | solution.py:34
  522.4 13.5 copy-start.5
  522.4 13.5 copy-start.8
  522.4 13.5 copy-start.9
  535.9 1108.2 %copy-start.4 = (s32[8,1024]{1,0:T(8,128)S(1)}, s32[8,1024]{1,0:T(8,128)}, u32[]{:S(2)}) copy-start(s32[8,1024]{1,0:T(8,128)} %param.23) | copy-start | bytes 98308
  542.3 4.6 copy-start.2
  559.7 4.6 copy-start.2
  577.0 4.6 copy-start.2
  594.3 4.6 copy-start.2
  611.6 4.6 copy-start.2
  628.9 4.6 copy-start.2
  646.2 4.6 copy-start.2
  663.5 4.6 copy-start.2
  854.0 4.6 copy-start.2
  940.6 4.6 copy-start.2
  1183.0 4.6 copy-start.2
  1269.5 4.6 copy-start.2
  1511.9 4.6 copy-start.2
  1598.5 4.6 copy-start.2
  (54 other events, 241.5 us)
Sparse Core Ops, SparseCore 0:
  9.2 39.0 all-gather.4
  50.2 38.7 all-gather.8
  90.6 279.5 all-gather.6
  371.9 143.2 all-gather.10
where the time goes:
time: 1670 us; the launch traced here: 1650 us
  matrix products  567 us (34%)
  waiting for transfers between devices  461 us (28%)
  local copies, waits for them, and re-layouts  328 us (20%)
  loops' own time  214 us (13%)
  other arithmetic  49 us (3%)
    all_gather x1, waiting for transfers between devices, local(): projected = lax.all_gather(local_pairs, 'cand', axis=1, tiled=True)  277 us
    dot_general x64, matrix products, score_block(): jnp.dot(block_rows, query_weight, preferred_element_type=jnp.float32)  185 us
    another operation x64, loops' own time, score_slot(): return lax.cond(is_live, score_block, empty_block, block_rows)  169 us
    dot_general x64, matrix products, score_block(): jnp.dot(merged, proj_hidden, preferred_element_type=jnp.float32)  163 us
    all_to_all x1, waiting for transfers between devices, local(): lax.all_to_all(outgoing, 'cand', split_axis=0, concat_axis=0, tiled=True)  140 us
    dot_general x64, matrix products, score_block(): jnp.einsum('hip,phd->ihd', weights, value_rows, preferred_element_type=jn...  116 us
    dot_general x64, matrix products, score_block(): jnp.dot(block_rows, gate_weight, preferred_element_type=jnp.float32)  89.5 us
    dynamic_slice x128, local copies, waits for them, and re-layouts, local(): lax.map(score_slot, (arrived.reshape(slot_count, BLOCK, model_width), req...  83.3 us
  transfers between devices with their start and end apart: 5, of which 4 were waited for; matrix products, arithmetic and copies ran while one was open for 3% of the time, Pallas kernels for 0%

commit v1 on v0

v1 whole, which is shorter than its diff:
```python
import math

import jax
import jax.numpy as jnp
from jax import lax
from jax.experimental import pallas as pl
from jax.experimental.pallas import tpu as pltpu
from jax.sharding import PartitionSpec as P

HEADS = 8
BLOCK = 128
EPSILON = 1e-05
AGE_SCALE = 48.0


def silu(value):
    half = 0.5 * value
    return half + half * jnp.tanh(half)


def pair_kernel(
    length_ref,
    history_ref,
    items_ref,
    history_weight_ref,
    candidate_weight_ref,
    output_weight_ref,
    hidden_weight_ref,
    gain_ref,
    score_weight_ref,
    logits_ref,
    query_ref,
    gate_ref,
    pairs_ref,
    attended_ref,
):
    request = pl.program_id(0)
    rows, width = items_ref.shape
    head = width // HEADS
    history_total = history_ref.shape[1]
    half_scale = 0.5 / math.sqrt(head)

    @pl.when(request == 0)
    def _():
        query_ref[...] = silu(
            jnp.dot(
                items_ref[...],
                candidate_weight_ref[:, :width],
                preferred_element_type=jnp.float32,
            )
        ).astype(jnp.bfloat16)
        gate_ref[...] = (
            silu(
                jnp.dot(
                    items_ref[...],
                    candidate_weight_ref[:, width:],
                    preferred_element_type=jnp.float32,
                )
            )
            * gain_ref[...]
        )

    length = length_ref[request]
    inverse = 1.0 / jnp.full((1, 1), length, jnp.int32).astype(jnp.float32)
    pairs_ref[:, :width] = silu(
        jnp.dot(
            history_ref[0], history_weight_ref[:, :width], preferred_element_type=jnp.float32
        )
    ).astype(jnp.bfloat16)
    live = lax.broadcasted_iota(jnp.int32, (history_total, width), 0) < length
    pairs_ref[:, width:] = jnp.where(
        live,
        silu(
            jnp.dot(
                history_ref[0], history_weight_ref[:, width:], preferred_element_type=jnp.float32
            )
        ),
        0.0,
    ).astype(jnp.bfloat16)
    for h in range(HEADS):
        part = slice(h * head, (h + 1) * head)
        scores = half_scale * lax.dot_general(
            query_ref[:, part],
            pairs_ref[:, part],
            (((1,), (1,)), ((), ())),
            preferred_element_type=jnp.float32,
        )
        weights = ((scores + scores * jnp.tanh(scores)) * inverse).astype(jnp.bfloat16)
        attended_ref[:, part] = jnp.dot(
            weights,
            pairs_ref[:, width + h * head : width + (h + 1) * head],
            preferred_element_type=jnp.float32,
        )
    attended = attended_ref[...]
    center = attended - jnp.mean(attended, axis=-1, keepdims=True)
    spread = jnp.mean(center * center, axis=-1, keepdims=True)
    normed = (center * lax.rsqrt(spread + EPSILON) * gate_ref[...]).astype(jnp.bfloat16)
    merged = (
        jnp.dot(normed, output_weight_ref[...], preferred_element_type=jnp.float32)
        + items_ref[...].astype(jnp.float32)
    ).astype(jnp.bfloat16)
    hidden = silu(
        jnp.dot(merged, hidden_weight_ref[...], preferred_element_type=jnp.float32)
    ).astype(jnp.bfloat16)
    logits_ref[0] = lax.dot_general(
        score_weight_ref[...],
        hidden,
        (((1,), (1,)), ((), ())),
        preferred_element_type=jnp.float32,
    )


def pair_logits(
    history, length, items, history_weight, candidate_weight, output_weight, hidden_weight, gain,
    score_weight,
):
    requests, history_total, width = history.shape
    rows = items.shape[0]
    whole = pl.BlockSpec(memory_space=pltpu.VMEM)
    return pl.pallas_call(
        pair_kernel,
        out_shape=jax.ShapeDtypeStruct((requests, score_weight.shape[0], rows), jnp.float32),
        grid=(requests,),
        in_specs=[
            pl.BlockSpec(memory_space=pltpu.SMEM),
            pl.BlockSpec((1, history_total, width), lambda i: (i, 0, 0)),
            whole, whole, whole, whole, whole, whole, whole,
        ],
        out_specs=pl.BlockSpec((1, score_weight.shape[0], rows), lambda i: (i, 0, 0)),
        scratch_shapes=[
            pltpu.VMEM((rows, width), jnp.bfloat16),
            pltpu.VMEM((rows, width), jnp.float32),
            pltpu.VMEM((history_total, 2 * width), jnp.bfloat16),
            pltpu.VMEM((rows, width), jnp.float32),
        ],
        compiler_params=pltpu.CompilerParams(vmem_limit_bytes=56 * 1024 * 1024),
    )(
        length, history, items, history_weight, candidate_weight, output_weight, hidden_weight,
        gain, score_weight,
    )


def blend(logits, candidate_count, block_shard, block_index, item_ages, item_blocks):
    shards = lax.axis_size("cand")
    mine = lax.axis_index("cand")
    requests, max_blocks = block_shard.shape
    per_scorer = max_blocks // shards
    logits = logits.reshape(shards, requests, -1, item_blocks, BLOCK)
    ids = lax.dynamic_slice_in_dim(
        block_shard * item_blocks + block_index, mine * per_scorer, per_scorer, 1
    )
    names = jnp.arange(shards * item_blocks, dtype=jnp.int32).reshape(shards, 1, 1, item_blocks, 1)
    picked = ids[None, :, :, None, None] == names
    first, second = (
        jnp.sum(jnp.where(picked, logits[:, :, None, c], 0.0), axis=(0, 3)) for c in (0, 1)
    )
    decays = jnp.exp(
        -item_ages.astype(jnp.float32).reshape(requests, per_scorer, BLOCK) / AGE_SCALE
    )
    blended = decays * first + (1.0 - decays) * second
    row_number = (mine * per_scorer + jnp.arange(per_scorer, dtype=jnp.int32))[
        None, :, None
    ] * BLOCK + jnp.arange(BLOCK, dtype=jnp.int32)[None, None, :]
    kept_rows = row_number < candidate_count[:, None, None]
    return jnp.where(kept_rows, blended, 0.0).reshape(requests, per_scorer * BLOCK)


def local(
    history,
    history_length,
    candidate_count,
    block_shard,
    block_index,
    item_table,
    item_ages,
    history_weight,
    candidate_weight,
    output_weight,
    hidden_weight,
    norm_gain,
    score_weight,
):
    proj = [
        lax.all_gather(weight, "req", axis=0, tiled=True)
        for weight in (history_weight, candidate_weight, output_weight, hidden_weight)
    ]
    full_history = lax.all_gather(history, "cand", axis=1, tiled=True)
    item_blocks = item_table.shape[0]
    logits = pair_logits(
        full_history,
        history_length,
        item_table.reshape(-1, item_table.shape[2]),
        *proj,
        norm_gain[None, :],
        score_weight,
    )
    logits = lax.all_gather(logits, "cand", axis=0, tiled=True)
    return blend(logits, candidate_count, block_shard, block_index, item_ages, item_blocks)


def solution(mesh):
    return jax.shard_map(
        local,
        mesh=mesh,
        in_specs=(
            P("req", "cand", None),
            P("req"),
            P("req"),
            P("req", None),
            P("req", None),
            P("cand", None, None),
            P("req", "cand"),
            P("req", None),
            P("req", None),
            P("req", None),
            P("req", None),
            P(),
            P(),
        ),
        out_specs=P("req", "cand"),
        check_vma=False,
    )
```

time: 1670 us -> 267 us (0.16)
  matrix products: 567 us -> 0 us
  local copies, waits for them, and re-layouts: 328 us -> 0.3 us
  waiting for transfers between devices: 461 us -> 177 us
  loops' own time: 214 us -> 0 us
  Pallas kernels: 0 us -> 48.1 us
  other arithmetic: 49 us -> 1.71 us
    dot_general x321 -> x0, matrix products: 567 us -> none  [the longest x64 185 us: score_block(): jnp.dot(block_rows, query_weight, preferred_element_type=jnp.float32)]
    another operation x65 -> x0, loops' own time: 214 us -> none  [the longest x64 169 us: score_slot(): return lax.cond(is_live, score_block, empty_block, block_rows)]
    all_gather x4, waiting for transfers between devices: 319 us -> 174 us  [the longest x3 92.2 us: local(): lax.all_gather(weight, 'req', axis=0, tiled=True)]
    all_to_all x1 -> x0, waiting for transfers between devices: 140 us -> none  [local(): lax.all_to_all(outgoing, 'cand', split_axis=0, concat_axis=0, tiled=True)]
    dynamic_slice x192 -> x1, local copies, waits for them, and re-layouts: 121 us -> 0.07 us  [blend(): lax.dynamic_slice_in_dim(block_shard * item_blocks + block_index, mine *...]
    squeeze x64 -> x0, local copies, waits for them, and re-layouts: 83 us -> none  [score_block(): pair_rows = lax.dynamic_index_in_dim(projected, request, 0, keepdims=False)]
    slice x66 -> x0, local copies, waits for them, and re-layouts: 71.4 us -> none  [the longest x64 67.2 us: score_block(): pair_rows[:, :model_width].reshape(history_total, HEADS, head_size)]
    pallas_call x0 -> x1, Pallas kernels: none -> 48.1 us  [pair_logits(): pl.pallas_call(pair_kernel, out_shape=jax.ShapeDtypeStruct((requests, sco...]
  transfers between devices with their start and end apart: 5 -> 4, of which waited for: 4 -> 4; matrix products, arithmetic and copies ran while one was open for 3% -> 0% of each run, Pallas kernels for 0% -> 0%
where the time goes in v1:
time: 267 us; the launch traced here: 264 us
  waiting for transfers between devices  177 us (66%)
  Pallas kernels  48.1 us (18%)
  blocking collectives  23.8 us (9%)
  between operations  13.2 us (5%)
    all_gather x3, waiting for transfers between devices, local(): lax.all_gather(weight, 'req', axis=0, tiled=True)  92.2 us
    all_gather x1, waiting for transfers between devices, local(): full_history = lax.all_gather(history, 'cand', axis=1, tiled=True)  81.8 us
    pallas_call x1, Pallas kernels, pair_logits(): pl.pallas_call(pair_kernel, out_shape=jax.ShapeDtypeStruct((requests, sco...  48.1 us
    all_gather x1, blocking collectives, local(): lax.all_gather(weight, 'req', axis=0, tiled=True)  13.1 us
    all_gather x1, blocking collectives, local(): logits = lax.all_gather(logits, 'cand', axis=0, tiled=True)  10.7 us
  transfers between devices with their start and end apart: 4, of which 4 were waited for; matrix products, arithmetic and copies ran while one was open for 0% of the time, Pallas kernels for 0%

profile of v1, /device:TPU:1, one launch (start us, length us, event | category | flops | bytes accessed | tf_op | source)
XLA Modules:
  0.0 263.8 jit_solution(11573889640386421367)
XLA Ops:
  6.5 0.0 all-gather.11.cloned.1.call-start
  6.5 0.7 all-gather.11.cloned.1.call-update
  7.3 0.0 all-gather.5.cloned.1.call-start
  7.3 0.7 all-gather.5.cloned.1.call-update
  8.0 0.0 all-gather.7.cloned.1.call-start
  8.1 0.7 all-gather.7.cloned.1.call-update
  8.7 0.0 all-gather.9.cloned.1.call-start
  8.8 0.5 all-gather.9.cloned.1.call-update
  9.3 0.7 multiply_add_fusion
  10.1 0.1 constant_dynamic-slice_fusion
  10.1 13.1 %all_gather.22.hidden_weight_ref = bf16[1024,256]{1,0:T(8,128)(2,1)} all-gather(bf16[128,256]{1,0:T(8,128)(2,1)} %param.23), channel_id=1, replica_groups=mesh['req'=8,'cand'=4] {'req'}, dimensions={0}, use_global_device_ids=true | all-gather | bytes 589824 | tf_op jit(solution)/shard_map/all_gather | solution.py:184
  23.2 0.1 add.56
  23.3 0.1 broadcast_compare_fusion
  23.4 16.3 %all-gather.11.cloned.1.call-done.output_weight_ref = bf16[1024,1024]{1,0:T(8,128)(2,1)} async-done(((bf16[128,1024]{1,0:T(8,128)(2,1)}), bf16[1024,1024]{1,0:T(8,128)(2,1)}) %all-gather.11.cloned.1.call-update) | async-done | bytes 2097168 | tf_op jit(solution)/shard_map/all_gather | solution.py:184
  39.7 81.8 %all-gather.5.cloned.1.call-done.history_ref = bf16[8,256,1024]{2,1,0:T(8,128)(2,1)} async-done(((bf16[8,64,1024]{2,1,0:T(8,128)(2,1)}), bf16[8,256,1024]{2,1,0:T(8,128)(2,1)}) %all-gather.5.cloned.1.call-update) | async-done | bytes 4194320 | tf_op jit(solution)/shard_map/all_gather | solution.py:187
  121.5 37.6 %all-gather.7.cloned.1.call-done.history_weight_ref = bf16[1024,2048]{1,0:T(8,128)(2,1)} async-done(((bf16[128,2048]{1,0:T(8,128)(2,1)}), bf16[1024,2048]{1,0:T(8,128)(2,1)}) %all-gather.7.cloned.1.call-update) | async-done | bytes 4194320 | tf_op jit(solution)/shard_map/all_gather | solution.py:184
  159.0 38.4 %all-gather.9.cloned.1.call-done.candidate_weight_ref = bf16[1024,2048]{1,0:T(8,128)(2,1)} async-done(((bf16[128,2048]{1,0:T(8,128)(2,1)}), bf16[1024,2048]{1,0:T(8,128)(2,1)}) %all-gather.9.cloned.1.call-update) | async-done | bytes 4194320 | tf_op jit(solution)/shard_map/all_gather | solution.py:184
  197.4 48.1 %shard_map.127 = f32[8,2,512]{2,1,0:T(2,128)} custom-call(s32[8]{0:T(128)} %length_ref.1, bf16[8,256,1024]{2,1,0:T(8,128)(2,1)} %all-gather.5.cloned.1.call-done.history_ref, bf16[512,1024]{1,0:T(8,128)(2,1)} %bitcast.21, bf16[1024,2048]{1,0:T(8,128)(2,1)} %all-gather.7.cloned.1.call-done.history_weight_ref, ...), custom_call_target="tpu_custom_call" | custom-call | tf_op jit(solution)/shard_map/pallas_call | solution.py:120
  245.5 10.7 %all_gather.23 = f32[32,2,512]{2,1,0:T(2,128)S(1)} all-gather(f32[8,2,512]{2,1,0:T(2,128)} %shard_map.127), channel_id=1, replica_groups=mesh['req'=8,'cand'=4] {'cand'}, dimensions={0}, use_global_device_ids=true | all-gather | bytes 163840 | tf_op jit(solution)/shard_map/all_gather | solution.py:197
  256.2 0.1 reshape.75
  256.4 0.2 select_reduce_fusion.1
  256.6 0.0 copy-done
  256.6 0.0 copy-done.1
  256.6 0.7 fusion.1
  (6 shorter events, 0.0 us)
Async XLA Ops:
  6.5 33.1 %all-gather.11.cloned.1.call-start = ((), (), s32[]{:S(2)}) async-start(), calls=%async_computation.3 | async-start | bytes 2359296 | tf_op jit(solution)/shard_map/all_gather | solution.py:184
  7.3 114.2 %all-gather.5.cloned.1.call-start = ((), (), s32[]{:S(2)}) async-start(), calls=%async_computation | async-start | bytes 5242880 | tf_op jit(solution)/shard_map/all_gather | solution.py:187
  8.0 151.0 %all-gather.7.cloned.1.call-start = ((), (), s32[]{:S(2)}) async-start(), calls=%async_computation.1 | async-start | bytes 4718592 | tf_op jit(solution)/shard_map/all_gather | solution.py:184
  8.7 188.6 %all-gather.9.cloned.1.call-start = ((), (), s32[]{:S(2)}) async-start(), calls=%async_computation.2 | async-start | bytes 4718592 | tf_op jit(solution)/shard_map/all_gather | solution.py:184
  197.4 59.2 %copy-start = (s32[8,1024]{1,0:T(8,128)S(1)}, s32[8,1024]{1,0:T(8,128)}, u32[]{:S(2)}) copy-start(s32[8,1024]{1,0:T(8,128)} %param.19) | copy-start | bytes 98308
  197.4 59.2 %copy-start.1 = (s32[8]{0:T(128)S(1)}, s32[8]{0:T(128)}, u32[]{:S(2)}) copy-start(s32[8]{0:T(128)} %param.15) | copy-start | bytes 100
Sparse Core Ops, SparseCore 0:
  9.2 30.3 all-gather.10
  41.2 80.1 all-gather.4
  123.4 35.6 all-gather.6
  160.8 36.5 all-gather.8

commit v2 on v1

v2 whole, which is shorter than its diff:
```python
import functools
import math

import jax
import jax.numpy as jnp
from jax import lax
from jax.experimental import pallas as pl
from jax.experimental.pallas import tpu as pltpu
from jax.sharding import PartitionSpec as P

HEADS = 8
BLOCK = 128
EPSILON = 1e-05
AGE_SCALE = 48.0


def silu(value):
    half = 0.5 * value
    return half + half * jnp.tanh(half)


MESH = pl.DeviceIdType.MESH


def pair_kernel(
    groups,
    shards,
    length_ref,
    history_ref,
    items_ref,
    history_shard_ref,
    candidate_shard_ref,
    output_shard_ref,
    hidden_shard_ref,
    gain_ref,
    score_weight_ref,
    logits_ref,
    events_ref,
    history_weight_ref,
    candidate_weight_ref,
    output_weight_ref,
    hidden_weight_ref,
    query_ref,
    gate_ref,
    pairs_ref,
    attended_ref,
    weight_send,
    weight_recv,
    pass_send,
    event_send,
    event_recv,
    logit_send,
    logit_recv,
    own_sem,
):
    group = lax.axis_index("req")
    shard = lax.axis_index("cand")
    partner = group + 1 - 2 * lax.rem(group, 2)
    requests, own_events, width = history_ref.shape
    history_total = events_ref.shape[1]
    head = width // HEADS
    half_scale = 0.5 / math.sqrt(head)
    weights = (
        (candidate_shard_ref, candidate_weight_ref),
        (history_shard_ref, history_weight_ref),
        (output_shard_ref, output_weight_ref),
        (hidden_shard_ref, hidden_weight_ref),
    )
    depth = history_shard_ref.shape[0]
    same_core = [lax.rem(group + 2 * d, groups) for d in range(1, groups // 2)]
    partner_core = [lax.rem(partner + 2 * d, groups) for d in range(1, groups // 2)]
    others = [lax.rem(shard + d, shards) for d in range(1, shards)]

    def rows_of(source):
        return pl.ds(pl.multiple_of(source * depth, depth), depth)

    def events_of(source):
        return pl.ds(pl.multiple_of(source * own_events, own_events), own_events)

    def weight_copy(w, target, source, send):
        part, full = weights[w]
        return pltpu.make_async_remote_copy(
            src_ref=part,
            dst_ref=full.at[rows_of(source)],
            send_sem=send,
            recv_sem=weight_recv.at[w, source],
            device_id={"req": target},
            device_id_type=MESH,
        )

    def pass_copy(w, k, source):
        full = weights[w][1]
        return pltpu.make_async_remote_copy(
            src_ref=full.at[rows_of(source)],
            dst_ref=full.at[rows_of(source)],
            send_sem=pass_send.at[w, k],
            recv_sem=weight_recv.at[w, source],
            device_id={"req": partner},
            device_id_type=MESH,
        )

    def event_copy(i, k, target, source):
        return pltpu.make_async_remote_copy(
            src_ref=history_ref.at[i],
            dst_ref=events_ref.at[i, events_of(source)],
            send_sem=event_send.at[i, k],
            recv_sem=event_recv.at[i, source],
            device_id={"cand": target},
            device_id_type=MESH,
        )

    def logit_copy(i, k, target, source):
        return pltpu.make_async_remote_copy(
            src_ref=logits_ref.at[source, i],
            dst_ref=logits_ref.at[source, i],
            send_sem=logit_send.at[i, k],
            recv_sem=logit_recv.at[i, source],
            device_id={"cand": target},
            device_id_type=MESH,
        )

    def own_weight(w):
        part, full = weights[w]
        return pltpu.make_async_copy(part, full.at[rows_of(group)], own_sem.at[w])

    def own_event(i):
        return pltpu.make_async_copy(
            history_ref.at[i], events_ref.at[i, events_of(shard)], own_sem.at[len(weights) + i]
        )

    barrier = pltpu.get_barrier_semaphore()
    for target in (*same_core, partner):
        pl.semaphore_signal(barrier, inc=1, device_id={"req": target}, device_id_type=MESH)
    for target in others:
        pl.semaphore_signal(barrier, inc=1, device_id={"cand": target}, device_id_type=MESH)
    pl.semaphore_wait(barrier, len(same_core) + 1 + len(others))

    for w in range(len(weights)):
        for k, target in enumerate(same_core):
            weight_copy(w, target, group, weight_send.at[w, k]).start()
        weight_copy(w, partner, group, weight_send.at[w, len(same_core)]).start()
        own_weight(w).start()

    @pl.loop(0, requests)
    def _(i):
        for k, target in enumerate(others):
            event_copy(i, k, target, shard).start()
        own_event(i).start()

    def pass_on(w):
        for k, source in enumerate(same_core):
            weight_copy(w, partner, source, weight_send.at[w, k]).wait_recv()
            pass_copy(w, k, source).start()

    def settle(w):
        own_weight(w).wait()
        for source in (partner, *partner_core):
            weight_copy(w, partner, source, weight_send.at[w, 0]).wait_recv()

    pass_on(0)
    settle(0)
    query_ref[...] = silu(
        jnp.dot(
            items_ref[...], candidate_weight_ref[:, :width], preferred_element_type=jnp.float32
        )
    ).astype(jnp.bfloat16)
    gate_ref[...] = (
        silu(
            jnp.dot(
                items_ref[...], candidate_weight_ref[:, width:], preferred_element_type=jnp.float32
            )
        )
        * gain_ref[...]
    )
    for w in range(1, len(weights)):
        pass_on(w)
    for w in range(1, len(weights)):
        settle(w)

    @pl.loop(0, requests)
    def _(i):
        own_event(i).wait()
        for k, source in enumerate(others):
            event_copy(i, k, source, source).wait_recv()
        length = length_ref[i]
        inverse = 1.0 / jnp.full((1, 1), length, jnp.int32).astype(jnp.float32)
        pairs_ref[:, :width] = silu(
            jnp.dot(
                events_ref[i], history_weight_ref[:, :width], preferred_element_type=jnp.float32
            )
        ).astype(jnp.bfloat16)
        live = lax.broadcasted_iota(jnp.int32, (history_total, width), 0) < length
        pairs_ref[:, width:] = jnp.where(
            live,
            silu(
                jnp.dot(
                    events_ref[i], history_weight_ref[:, width:], preferred_element_type=jnp.float32
                )
            ),
            0.0,
        ).astype(jnp.bfloat16)
        for h in range(HEADS):
            part = slice(h * head, (h + 1) * head)
            scores = half_scale * lax.dot_general(
                query_ref[:, part],
                pairs_ref[:, part],
                (((1,), (1,)), ((), ())),
                preferred_element_type=jnp.float32,
            )
            mixed = ((scores + scores * jnp.tanh(scores)) * inverse).astype(jnp.bfloat16)
            attended_ref[:, part] = jnp.dot(
                mixed,
                pairs_ref[:, width + h * head : width + (h + 1) * head],
                preferred_element_type=jnp.float32,
            )

        @pl.when(i > 0)
        def _():
            for k, target in enumerate(others):
                logit_copy(i - 1, k, target, shard).start()

        attended = attended_ref[...]
        center = attended - jnp.mean(attended, axis=-1, keepdims=True)
        spread = jnp.mean(center * center, axis=-1, keepdims=True)
        normed = (center * lax.rsqrt(spread + EPSILON) * gate_ref[...]).astype(jnp.bfloat16)
        merged = (
            jnp.dot(normed, output_weight_ref[...], preferred_element_type=jnp.float32)
            + items_ref[...].astype(jnp.float32)
        ).astype(jnp.bfloat16)
        hidden = silu(
            jnp.dot(merged, hidden_weight_ref[...], preferred_element_type=jnp.float32)
        ).astype(jnp.bfloat16)
        logits_ref[shard, i] = lax.dot_general(
            score_weight_ref[...],
            hidden,
            (((1,), (1,)), ((), ())),
            preferred_element_type=jnp.float32,
        )

    for w in range(len(weights)):
        for k, target in enumerate((*same_core, partner)):
            weight_copy(w, target, group, weight_send.at[w, k]).wait_send()
        for k, source in enumerate(same_core):
            pass_copy(w, k, source).wait_send()

    @pl.loop(0, requests)
    def _(i):
        for k, target in enumerate(others):
            event_copy(i, k, target, shard).wait_send()

    for k, target in enumerate(others):
        logit_copy(requests - 1, k, target, shard).start()

    @pl.loop(0, requests)
    def _(i):
        for k, target in enumerate(others):
            logit_copy(i, k, target, shard).wait_send()
            logit_copy(i, k, target, target).wait_recv()


def pair_logits(
    history, length, items, history_weight, candidate_weight, output_weight, hidden_weight, gain,
    score_weight,
):
    requests, own_events, width = history.shape
    rows = items.shape[0]
    groups, shards = lax.axis_size("req"), lax.axis_size("cand")
    history_total = own_events * shards
    whole = pl.BlockSpec(memory_space=pltpu.VMEM)
    apart = pl.BlockSpec(memory_space=pl.ANY)
    weights = (history_weight, candidate_weight, output_weight, hidden_weight)
    count = len(weights)
    return pl.pallas_call(
        functools.partial(pair_kernel, groups, shards),
        out_shape=jax.ShapeDtypeStruct((shards, requests, score_weight.shape[0], rows), jnp.float32),
        in_specs=[
            pl.BlockSpec(memory_space=pltpu.SMEM),
            apart, whole, apart, apart, apart, apart, whole, whole,
        ],
        out_specs=whole,
        scratch_shapes=[
            pltpu.VMEM((requests, history_total, width), jnp.bfloat16),
            *(
                pltpu.VMEM((weight.shape[0] * groups, weight.shape[1]), jnp.bfloat16)
                for weight in weights
            ),
            pltpu.VMEM((rows, width), jnp.bfloat16),
            pltpu.VMEM((rows, width), jnp.float32),
            pltpu.VMEM((history_total, 2 * width), jnp.bfloat16),
            pltpu.VMEM((rows, width), jnp.float32),
            pltpu.SemaphoreType.DMA((count, groups // 2)),
            pltpu.SemaphoreType.DMA((count, groups)),
            pltpu.SemaphoreType.DMA((count, groups // 2)),
            pltpu.SemaphoreType.DMA((requests, shards)),
            pltpu.SemaphoreType.DMA((requests, shards)),
            pltpu.SemaphoreType.DMA((requests, shards)),
            pltpu.SemaphoreType.DMA((requests, shards)),
            pltpu.SemaphoreType.DMA((count + requests,)),
        ],
        compiler_params=pltpu.CompilerParams(
            collective_id=0, has_side_effects=True, vmem_limit_bytes=58 * 1024 * 1024
        ),
    )(
        length, history, items, history_weight, candidate_weight, output_weight, hidden_weight,
        gain, score_weight,
    )


def blend(logits, candidate_count, block_shard, block_index, item_ages, item_blocks):
    shards = lax.axis_size("cand")
    mine = lax.axis_index("cand")
    requests, max_blocks = block_shard.shape
    per_scorer = max_blocks // shards
    logits = logits.reshape(shards, requests, -1, item_blocks, BLOCK)
    ids = lax.dynamic_slice_in_dim(
        block_shard * item_blocks + block_index, mine * per_scorer, per_scorer, 1
    )
    names = jnp.arange(shards * item_blocks, dtype=jnp.int32).reshape(shards, 1, 1, item_blocks, 1)
    picked = ids[None, :, :, None, None] == names
    first, second = (
        jnp.sum(jnp.where(picked, logits[:, :, None, c], 0.0), axis=(0, 3)) for c in (0, 1)
    )
    decays = jnp.exp(
        -item_ages.astype(jnp.float32).reshape(requests, per_scorer, BLOCK) / AGE_SCALE
    )
    blended = decays * first + (1.0 - decays) * second
    row_number = (mine * per_scorer + jnp.arange(per_scorer, dtype=jnp.int32))[
        None, :, None
    ] * BLOCK + jnp.arange(BLOCK, dtype=jnp.int32)[None, None, :]
    kept_rows = row_number < candidate_count[:, None, None]
    return jnp.where(kept_rows, blended, 0.0).reshape(requests, per_scorer * BLOCK)


def local(
    history,
    history_length,
    candidate_count,
    block_shard,
    block_index,
    item_table,
    item_ages,
    history_weight,
    candidate_weight,
    output_weight,
    hidden_weight,
    norm_gain,
    score_weight,
):
    item_blocks = item_table.shape[0]
    logits = pair_logits(
        history,
        history_length,
        item_table.reshape(-1, item_table.shape[2]),
        history_weight,
        candidate_weight,
        output_weight,
        hidden_weight,
        norm_gain[None, :],
        score_weight,
    )
    return blend(logits, candidate_count, block_shard, block_index, item_ages, item_blocks)


def solution(mesh):
    return jax.shard_map(
        local,
        mesh=mesh,
        in_specs=(
            P("req", "cand", None),
            P("req"),
            P("req"),
            P("req", None),
            P("req", None),
            P("cand", None, None),
            P("req", "cand"),
            P("req", None),
            P("req", None),
            P("req", None),
            P("req", None),
            P(),
            P(),
        ),
        out_specs=P("req", "cand"),
        check_vma=False,
    )
```

time: 267 us -> 118 us (0.44); the launches traced: 264 us -> 118 us
  waiting for transfers between devices: 177 us -> 0 us
  Pallas kernels: 48.1 us -> 114 us
  blocking collectives: 23.8 us -> 0 us
  between operations: 13.2 us -> 0.07 us
    all_gather x4 -> x0, waiting for transfers between devices: 174 us -> none  [the longest x3 92.2 us: local(): lax.all_gather(weight, 'req', axis=0, tiled=True)]
    pallas_call x1, Pallas kernels: 48.1 us -> 114 us  [pair_logits(): pl.pallas_call(functools.partial(pair_kernel, groups, shards), out_shape=...]
    all_gather x2 -> x0, blocking collectives: 23.8 us -> none  [the longest x1 13.1 us: local(): lax.all_gather(weight, 'req', axis=0, tiled=True)]
  transfers between devices with their start and end apart: 4 -> 0, of which waited for: 4 -> 0; matrix products, arithmetic and copies ran while one was open for 0% -> 0% of each run, Pallas kernels for 0% -> 0%
where the time goes in v2:
time: 118 us
  Pallas kernels  114 us (97%)
  local copies, waits for them, and re-layouts  2.51 us (2%)
    pallas_call x1, Pallas kernels, pair_logits(): pl.pallas_call(functools.partial(pair_kernel, groups, shards), out_shape=...  114 us

profile of v2, /device:TPU:1, one launch (start us, length us, event | category | flops | bytes accessed | tf_op | source)
XLA Modules:
  0.0 118.1 jit_solution(3486973946417464285)
XLA Ops:
  0.0 114.5 %shard_map.127 = f32[4,8,2,512]{3,2,1,0:T(2,128)} custom-call(s32[8]{0:T(128)} %length_ref.1, bf16[8,64,1024]{2,1,0:T(8,128)(2,1)} %history_ref.1, bf16[512,1024]{1,0:T(8,128)(2,1)} %bitcast.21, bf16[128,2048]{1,0:T(8,128)(2,1)} %history_shard_ref.1, bf16[128,2048]{1,0:T(8,128)(2,1)} %candidate_shard_ref.1, bf16[128,1024]{1,0:T(8,128)(2,1)} %output_shard_ref.1, ...), custom_call_target="tpu_custom_call" | custom-call | tf_op jit(solution)/shard_map/pallas_call | solution.py:273
  114.5 1.0 reshape.75
  115.5 0.0 copy-start.1
  115.6 0.0 copy-start.2
  115.6 0.6 copy-done.1
  116.2 0.0 copy-done.2
  116.3 0.1 constant_dynamic-slice_fusion
  116.3 0.1 broadcast_compare_fusion
  116.4 0.0 copy-start
  116.4 0.2 select_reduce_fusion.1
  116.7 0.1 add.56
  116.7 0.0 copy-start.3
  116.7 0.4 copy-done
  117.2 0.2 copy-done.3
  117.4 0.7 fusion.1
  (5 shorter events, 0.0 us)
Async XLA Ops:
  115.5 0.7 copy-start.1
  115.6 0.7 copy-start.2
  116.4 0.8 copy-start
  116.7 0.7 copy-start.3

commit v3 on v2

--- a/solution.py
+++ b/solution.py
@@ -47,6 +47,7 @@
     weight_send,
     weight_recv,
     pass_send,
+    turn_send,
     event_send,
     event_recv,
     logit_send,
@@ -67,9 +68,19 @@
         (hidden_shard_ref, hidden_weight_ref),
     )
     depth = history_shard_ref.shape[0]
-    same_core = [lax.rem(group + 2 * d, groups) for d in range(1, groups // 2)]
-    partner_core = [lax.rem(partner + 2 * d, groups) for d in range(1, groups // 2)]
+    half = groups // 2
+    row, core = lax.div(group, half), lax.rem(group, 2)
+    across = lax.rem(group + half, groups)
+    beside = [row * half + lax.rem(group - row * half + 2 * d, half) for d in range(1, half // 2)]
+    diagonal = [lax.rem(source + half, groups) for source in beside]
+    near = (*beside, across)
+    same_core = (*near, *diagonal)
+    partner_core = [source + partner - group for source in same_core]
     others = [lax.rem(shard + d, shards) for d in range(1, shards)]
+    last = shards - 1
+    relays = ((1, last, 0), (last - 1, 0, last)) if shards > 2 else ()
+    lead = requests // 2
+    ahead = lead // 2
 
     def rows_of(source):
         return pl.ds(pl.multiple_of(source * depth, depth), depth)
@@ -99,6 +110,47 @@
             device_id_type=MESH,
         )
 
+    def turn_copy(w, k):
+        full = weights[w][1]
+        source = beside[k] + core * (across - beside[k])
+        target = across + core * (beside[k] - across)
+        return pltpu.make_async_remote_copy(
+            src_ref=full.at[rows_of(source)],
+            dst_ref=full.at[rows_of(source)],
+            send_sem=turn_send.at[w, k],
+            recv_sem=weight_recv.at[w, source],
+            device_id={"req": target},
+            device_id_type=MESH,
+        )
+
+    def relay_copy(i, k):
+        _, source, target = relays[k]
+        return pltpu.make_async_remote_copy(
+            src_ref=events_ref.at[i, events_of(source)],
+            dst_ref=events_ref.at[i, events_of(source)],
+            send_sem=event_send.at[i, len(others) + k],
+            recv_sem=event_recv.at[i, source],
+            device_id={"cand": target},
+            device_id_type=MESH,
+        )
+
+    def is_far(target):
+        return (shards > 2) & (jnp.abs(target - shard) == last)
+
+    def is_relayed(source):
+        flag = shard < 0
+        for middle, start, _ in relays:
+            flag = flag | ((shard == middle) & (source == start))
+        return flag
+
+    def relay(i):
+        for k, (middle, source, _) in enumerate(relays):
+
+            @pl.when(shard == middle)
+            def _():
+                event_copy(i, 0, 0, source).wait_recv()
+                relay_copy(i, k).start()
+
     def event_copy(i, k, target, source):
         return pltpu.make_async_remote_copy(
             src_ref=history_ref.at[i],
@@ -129,35 +181,54 @@
         )
 
     barrier = pltpu.get_barrier_semaphore()
-    for target in (*same_core, partner):
+    for target in (*near, partner):
         pl.semaphore_signal(barrier, inc=1, device_id={"req": target}, device_id_type=MESH)
     for target in others:
         pl.semaphore_signal(barrier, inc=1, device_id={"cand": target}, device_id_type=MESH)
-    pl.semaphore_wait(barrier, len(same_core) + 1 + len(others))
-
-    for w in range(len(weights)):
-        for k, target in enumerate(same_core):
+    pl.semaphore_wait(barrier, len(near) + 1 + len(others))
+
+    def send(w):
+        for k, target in enumerate((*near, partner)):
             weight_copy(w, target, group, weight_send.at[w, k]).start()
-        weight_copy(w, partner, group, weight_send.at[w, len(same_core)]).start()
         own_weight(w).start()
+
+    send(0)
+    send(1)
 
     @pl.loop(0, requests)
     def _(i):
         for k, target in enumerate(others):
-            event_copy(i, k, target, shard).start()
+
+            @pl.when(jnp.logical_not(is_far(target)))
+            def _():
+                event_copy(i, k, target, shard).start()
+
         own_event(i).start()
 
-    def pass_on(w):
-        for k, source in enumerate(same_core):
-            weight_copy(w, partner, source, weight_send.at[w, k]).wait_recv()
-            pass_copy(w, k, source).start()
+    def pass_on(w, sources, first):
+        for k, source in enumerate(sources):
+            pass_copy(w, first + k, source).start()
+
+    def arrive(w, sources):
+        for source in sources:
+            weight_copy(w, partner, source, weight_send.at[w, 0]).wait_recv()
+
+    def turn(w):
+        arrive(w, near)
+        for k in range(len(beside)):
+            turn_copy(w, k).start()
+        pass_on(w, near, 0)
 
     def settle(w):
+        arrive(w, diagonal)
+        pass_on(w, diagonal, len(near))
         own_weight(w).wait()
-        for source in (partner, *partner_core):
-            weight_copy(w, partner, source, weight_send.at[w, 0]).wait_recv()
-
-    pass_on(0)
+        arrive(w, (partner, *partner_core))
+
+    turn(0)
+    for w in range(2, len(weights)):
+        send(w)
+    turn(1)
     settle(0)
     query_ref[...] = silu(
         jnp.dot(
@@ -172,16 +243,30 @@
         )
         * gain_ref[...]
     )
-    for w in range(1, len(weights)):
-        pass_on(w)
-    for w in range(1, len(weights)):
+    relay(0)
+    settle(1)
+    for w in range(2, len(weights)):
+        turn(w)
+    for i in range(1, ahead):
+        relay(i)
+    for w in range(2, len(weights)):
         settle(w)
+    for i in range(max(1, ahead), lead):
+        relay(i)
 
     @pl.loop(0, requests)
     def _(i):
+        @pl.when((i >= lead - ahead) & (i + ahead < requests))
+        def _():
+            relay(i + ahead)
+
         own_event(i).wait()
         for k, source in enumerate(others):
-            event_copy(i, k, source, source).wait_recv()
+
+            @pl.when(jnp.logical_not(is_relayed(source)))
+            def _():
+                event_copy(i, k, source, source).wait_recv()
+
         length = length_ref[i]
         inverse = 1.0 / jnp.full((1, 1), length, jnp.int32).astype(jnp.float32)
         pairs_ref[:, :width] = silu(
@@ -238,15 +323,26 @@
         )
 
     for w in range(len(weights)):
-        for k, target in enumerate((*same_core, partner)):
+        for k, target in enumerate((*near, partner)):
             weight_copy(w, target, group, weight_send.at[w, k]).wait_send()
         for k, source in enumerate(same_core):
             pass_copy(w, k, source).wait_send()
+        for k in range(len(beside)):
+            turn_copy(w, k).wait_send()
 
     @pl.loop(0, requests)
     def _(i):
         for k, target in enumerate(others):
-            event_copy(i, k, target, shard).wait_send()
+
+            @pl.when(jnp.logical_not(is_far(target)))
+            def _():
+                event_copy(i, k, target, shard).wait_send()
+
+        for k, (middle, _, _) in enumerate(relays):
+
+            @pl.when(shard == middle)
+            def _():
+                relay_copy(i, k).wait_send()
 
     for k, target in enumerate(others):
         logit_copy(requests - 1, k, target, shard).start()
@@ -291,7 +387,8 @@
             pltpu.SemaphoreType.DMA((count, groups // 2)),
             pltpu.SemaphoreType.DMA((count, groups)),
             pltpu.SemaphoreType.DMA((count, groups // 2)),
-            pltpu.SemaphoreType.DMA((requests, shards)),
+            pltpu.SemaphoreType.DMA((count, groups // 2)),
+            pltpu.SemaphoreType.DMA((requests, shards + 1)),
             pltpu.SemaphoreType.DMA((requests, shards)),
             pltpu.SemaphoreType.DMA((requests, shards)),
             pltpu.SemaphoreType.DMA((requests, shards)),

time: 118 us -> 109 us (0.924); the launches traced: 118 us -> 108 us
  Pallas kernels: 114 us -> 104 us
    pallas_call x1, Pallas kernels: 114 us -> 104 us  [pair_logits(): pl.pallas_call(functools.partial(pair_kernel, groups, shards), out_shape=...]
where the time goes in v3:
time: 109 us; the launch traced here: 108 us
  Pallas kernels  104 us (95%)
  local copies, waits for them, and re-layouts  2.51 us (2%)
    pallas_call x1, Pallas kernels, pair_logits(): pl.pallas_call(functools.partial(pair_kernel, groups, shards), out_shape=...  104 us

profile of v3, /device:TPU:1, one launch (start us, length us, event | category | flops | bytes accessed | tf_op | source)
XLA Modules:
  0.0 107.5 jit_solution(2224930957571086352)
XLA Ops:
  0.0 103.9 %shard_map.127 = f32[4,8,2,512]{3,2,1,0:T(2,128)} custom-call(s32[8]{0:T(128)} %length_ref.1, bf16[8,64,1024]{2,1,0:T(8,128)(2,1)} %history_ref.1, bf16[512,1024]{1,0:T(8,128)(2,1)} %bitcast.21, bf16[128,2048]{1,0:T(8,128)(2,1)} %history_shard_ref.1, bf16[128,2048]{1,0:T(8,128)(2,1)} %candidate_shard_ref.1, bf16[128,1024]{1,0:T(8,128)(2,1)} %output_shard_ref.1, ...), custom_call_target="tpu_custom_call" | custom-call | tf_op jit(solution)/shard_map/pallas_call | solution.py:369
  103.9 1.0 reshape.75
  105.0 0.0 copy-start.1
  105.0 0.0 copy-start.2
  105.0 0.6 copy-done.1
  105.7 0.0 copy-done.2
  105.7 0.1 constant_dynamic-slice_fusion
  105.8 0.1 broadcast_compare_fusion
  105.8 0.0 copy-start
  105.9 0.2 select_reduce_fusion.1
  106.1 0.1 add.56
  106.2 0.0 copy-start.3
  106.2 0.4 copy-done
  106.6 0.2 copy-done.3
  106.8 0.7 fusion.1
  (5 shorter events, 0.0 us)
Async XLA Ops:
  105.0 0.7 copy-start.1
  105.0 0.7 copy-start.2
  105.8 0.8 copy-start
  106.2 0.7 copy-start.3

commit v4 on v3

--- a/solution.py
+++ b/solution.py
@@ -243,23 +243,7 @@
         )
         * gain_ref[...]
     )
-    relay(0)
-    settle(1)
-    for w in range(2, len(weights)):
-        turn(w)
-    for i in range(1, ahead):
-        relay(i)
-    for w in range(2, len(weights)):
-        settle(w)
-    for i in range(max(1, ahead), lead):
-        relay(i)
-
-    @pl.loop(0, requests)
-    def _(i):
-        @pl.when((i >= lead - ahead) & (i + ahead < requests))
-        def _():
-            relay(i + ahead)
-
+    def project(i):
         own_event(i).wait()
         for k, source in enumerate(others):
 
@@ -267,15 +251,13 @@
             def _():
                 event_copy(i, k, source, source).wait_recv()
 
-        length = length_ref[i]
-        inverse = 1.0 / jnp.full((1, 1), length, jnp.int32).astype(jnp.float32)
-        pairs_ref[:, :width] = silu(
+        pairs_ref[i, :, :width] = silu(
             jnp.dot(
                 events_ref[i], history_weight_ref[:, :width], preferred_element_type=jnp.float32
             )
         ).astype(jnp.bfloat16)
-        live = lax.broadcasted_iota(jnp.int32, (history_total, width), 0) < length
-        pairs_ref[:, width:] = jnp.where(
+        live = lax.broadcasted_iota(jnp.int32, (history_total, width), 0) < length_ref[i]
+        pairs_ref[i, :, width:] = jnp.where(
             live,
             silu(
                 jnp.dot(
@@ -284,18 +266,47 @@
             ),
             0.0,
         ).astype(jnp.bfloat16)
+    relay(0)
+    settle(1)
+    for i in range(1, ahead):
+        relay(i)
+    ready = 0
+    for w in range(2, len(weights)):
+        turn(w)
+        for i in range(ready, ready + lead // 4):
+            project(i)
+        ready += lead // 4
+    for i in range(ahead, lead):
+        relay(i)
+    for i in range(ready, lead):
+        project(i)
+    for w in range(2, len(weights)):
+        settle(w)
+
+    @pl.loop(0, requests)
+    def _(i):
+        @pl.when((i >= lead - ahead) & (i + ahead < requests))
+        def _():
+            relay(i + ahead)
+
+        @pl.when(i >= lead)
+        def _():
+            project(i)
+
+        length = length_ref[i]
+        inverse = 1.0 / jnp.full((1, 1), length, jnp.int32).astype(jnp.float32)
         for h in range(HEADS):
             part = slice(h * head, (h + 1) * head)
             scores = half_scale * lax.dot_general(
                 query_ref[:, part],
-                pairs_ref[:, part],
+                pairs_ref[i, :, part],
                 (((1,), (1,)), ((), ())),
                 preferred_element_type=jnp.float32,
             )
             mixed = ((scores + scores * jnp.tanh(scores)) * inverse).astype(jnp.bfloat16)
             attended_ref[:, part] = jnp.dot(
                 mixed,
-                pairs_ref[:, width + h * head : width + (h + 1) * head],
+                pairs_ref[i, :, width + h * head : width + (h + 1) * head],
                 preferred_element_type=jnp.float32,
             )
 
@@ -382,7 +393,7 @@
             ),
             pltpu.VMEM((rows, width), jnp.bfloat16),
             pltpu.VMEM((rows, width), jnp.float32),
-            pltpu.VMEM((history_total, 2 * width), jnp.bfloat16),
+            pltpu.VMEM((requests, history_total, 2 * width), jnp.bfloat16),
             pltpu.VMEM((rows, width), jnp.float32),
             pltpu.SemaphoreType.DMA((count, groups // 2)),
             pltpu.SemaphoreType.DMA((count, groups)),

time: 109 us -> 118 us (1.083)
  Pallas kernels: 104 us -> 113 us
    pallas_call x1, Pallas kernels: 104 us -> 113 us  [pair_logits(): pl.pallas_call(functools.partial(pair_kernel, groups, shards), out_shape=...]
where the time goes in v4:
time: 118 us; the launch traced here: 117 us
  Pallas kernels  113 us (96%)
  local copies, waits for them, and re-layouts  2.51 us (2%)
    pallas_call x1, Pallas kernels, pair_logits(): pl.pallas_call(functools.partial(pair_kernel, groups, shards), out_shape=...  113 us

profile of v4, /device:TPU:1, one launch (start us, length us, event | category | flops | bytes accessed | tf_op | source)
XLA Modules:
  0.0 116.5 jit_solution(10562095469207183295)
XLA Ops:
  0.0 113.0 %shard_map.127 = f32[4,8,2,512]{3,2,1,0:T(2,128)} custom-call(s32[8]{0:T(128)} %length_ref.1, bf16[8,64,1024]{2,1,0:T(8,128)(2,1)} %history_ref.1, bf16[512,1024]{1,0:T(8,128)(2,1)} %bitcast.21, bf16[128,2048]{1,0:T(8,128)(2,1)} %history_shard_ref.1, bf16[128,2048]{1,0:T(8,128)(2,1)} %candidate_shard_ref.1, bf16[128,1024]{1,0:T(8,128)(2,1)} %output_shard_ref.1, ...), custom_call_target="tpu_custom_call" | custom-call | tf_op jit(solution)/shard_map/pallas_call | solution.py:380
  113.0 1.0 reshape.75
  114.0 0.0 copy-start.1
  114.0 0.0 copy-start.2
  114.1 0.6 copy-done.1
  114.7 0.0 copy-done.2
  114.7 0.1 constant_dynamic-slice_fusion
  114.8 0.1 broadcast_compare_fusion
  114.9 0.0 copy-start
  114.9 0.2 select_reduce_fusion.1
  115.1 0.1 add.56
  115.2 0.0 copy-start.3
  115.2 0.4 copy-done
  115.6 0.2 copy-done.3
  115.9 0.7 fusion.1
  (5 shorter events, 0.0 us)
Async XLA Ops:
  114.0 0.7 copy-start.1
  114.0 0.7 copy-start.2
  114.9 0.8 copy-start
  115.2 0.7 copy-start.3
